TPU v7x, 32 devices: a whole 2x2x4 slice. The times are simulated.
32 devices in a mesh: groups: 2 (over x), dp: 8 (over z, y), expert: 2 (over core).
Axes of the slice: x: 2, y: 2, z: 4, core: 2. Of those that a mesh axis runs over, the one named last changes fastest.
Arguments:
- tokens: bfloat16 [128, 4096], P(('groups', 'dp', 'expert')), parts along dimension 0, may hold values from -6 to 6
- cotangent: bfloat16 [128, 4096], P(('groups', 'dp', 'expert')), parts along dimension 0, may hold values from -6 to 6
- routing: int32 [128, 2], P(('groups', 'dp', 'expert')), parts along dimension 0, may hold values from 0 to 7, as said below
- gate_first: int32 [128], P(('groups', 'dp', 'expert')), parts along dimension 0, may hold values from 1 to 1023
- gate_weight: bfloat16 [4096, 65536], P(None, ('dp', 'expert')), may hold values from -0.09375 to 0.09375
- up_weight: bfloat16 [4096, 65536], P(None, ('dp', 'expert')), may hold values from -0.09375 to 0.09375
- down_weight: bfloat16 [65536, 4096], P(('dp', 'expert')), may hold values from -0.0625 to 0.0625
Outputs:
- mixed: bfloat16 [128, 4096], P(('groups', 'dp', 'expert')), parts along dimension 0
- token_grad: bfloat16 [128, 4096], P(('groups', 'dp', 'expert')), parts along dimension 0
- gate_grad: float32 [128, 2], P(('groups', 'dp', 'expert')), parts along dimension 0
There are 2 independent parts, one for each index of `groups`. A program takes and returns all parts, laid end to end along the dimension named above; an argument that names none is the same for every part. Nothing has to cross between parts.
Inputs may be any that keep to these rules, and one draw needn't show every extreme that they name: `routing`: the two experts of a token differ. Among the 4 tokens of one device (aligned blocks of 4 rows) no expert is named more than 2 times, and one expert is named exactly 2 times in every such block.
All inputs are finite; a program needn't handle non-finite values.
Results may differ from a plain program's by a relative error of at most 0.014.
Values may be sent and summed in bfloat16 or wider, within the bound.
A program may use at most 192 MiB of HBM per device.

v0:
```python
import jax
import jax.numpy as jnp
from jax import lax
from jax.sharding import PartitionSpec as P

E = 8


def expert_rows(got_x, got_dy, got_w, gate_weight, up_weight, down_weight):
    gate_pre = jnp.dot(got_x, gate_weight, preferred_element_type=jnp.float32)
    up_pre = jnp.dot(got_x, up_weight, preferred_element_type=jnp.float32)
    sig_gate = jax.nn.sigmoid(gate_pre)
    silu_gate = gate_pre * sig_gate
    hidden = (silu_gate * up_pre).astype(jnp.bfloat16)
    part_out = jnp.dot(hidden, down_weight, preferred_element_type=jnp.float32)
    d_hidden = got_w[:, None] * jnp.dot(got_dy, down_weight.T, preferred_element_type=jnp.float32)
    d_gate = (d_hidden * up_pre * sig_gate * (1.0 + gate_pre * (1.0 - sig_gate))).astype(
        jnp.bfloat16
    )
    d_up = (d_hidden * silu_gate).astype(jnp.bfloat16)
    part_grad = jnp.dot(d_gate, gate_weight.T, preferred_element_type=jnp.float32)
    part_grad = part_grad + jnp.dot(d_up, up_weight.T, preferred_element_type=jnp.float32)
    return (part_out.astype(jnp.bfloat16), part_grad.astype(jnp.bfloat16))


def on_device(tokens, cotangent, routing, gate_first, gate_weight, up_weight, down_weight):
    devices = lax.axis_size(("dp", "expert"))
    group_size = devices // E
    tok_rows = tokens.shape[0]
    width = tokens.shape[1]
    capacity = tok_rows // 2
    expert_ids = jnp.arange(E, dtype=jnp.int32)
    first_hot = (routing[:, 0:1] == expert_ids[None, :]).astype(jnp.int32)
    second_hot = (routing[:, 1:2] == expert_ids[None, :]).astype(jnp.int32)
    rank_rows = jnp.cumsum(first_hot + second_hot, axis=0) - 1
    slot_ids = jnp.arange(capacity, dtype=jnp.int32)
    slot_hot = (rank_rows[:, :, None] == slot_ids[None, None, :]).astype(jnp.float32)
    pick_first = first_hot[:, :, None].astype(jnp.float32) * slot_hot
    pick_second = second_hot[:, :, None].astype(jnp.float32) * slot_hot
    picked = pick_first + pick_second
    share_first = gate_first.astype(jnp.float32) / 1024.0
    share_second = (1024 - gate_first).astype(jnp.float32) / 1024.0
    picked_low = picked.astype(jnp.bfloat16)
    send_x = jnp.einsum(
        "tec,td->ecd", picked_low, tokens, preferred_element_type=jnp.float32
    ).astype(jnp.bfloat16)
    send_dy = jnp.einsum(
        "tec,td->ecd", picked_low, cotangent, preferred_element_type=jnp.float32
    ).astype(jnp.bfloat16)
    weighted = pick_first * share_first[:, None, None] + pick_second * share_second[:, None, None]
    send_w = jnp.sum(weighted, axis=0)
    out_x = jnp.repeat(send_x, group_size, axis=0)
    out_dy = jnp.repeat(send_dy, group_size, axis=0)
    out_w = jnp.repeat(send_w, group_size, axis=0)
    recv_x, recv_dy, recv_w = (
        lax.all_to_all(out_x, ("dp", "expert"), split_axis=0, concat_axis=0, tiled=True),
        lax.all_to_all(out_dy, ("dp", "expert"), split_axis=0, concat_axis=0, tiled=True),
        lax.all_to_all(
            out_w.astype(jnp.bfloat16), ("dp", "expert"), split_axis=0, concat_axis=0, tiled=True
        ).astype(out_w.dtype),
    )
    got_x = recv_x.reshape(devices * capacity, width)
    got_dy = recv_dy.reshape(devices * capacity, width)
    got_w = recv_w.reshape(devices * capacity)
    part_out, part_grad = expert_rows(got_x, got_dy, got_w, gate_weight, up_weight, down_weight)
    back_out, back_grad = (
        lax.all_to_all(
            part_out.reshape(devices, capacity, width),
            ("dp", "expert"),
            split_axis=0,
            concat_axis=0,
            tiled=True,
        ),
        lax.all_to_all(
            part_grad.reshape(devices, capacity, width),
            ("dp", "expert"),
            split_axis=0,
            concat_axis=0,
            tiled=True,
        ),
    )
    summed_out = jnp.sum(
        back_out.astype(jnp.float32).reshape(E, group_size, capacity, width), axis=1
    )
    summed_grad = jnp.sum(
        back_grad.astype(jnp.float32).reshape(E, group_size, capacity, width), axis=1
    )
    rank_first = jnp.take_along_axis(rank_rows, routing[:, 0:1], axis=1)[:, 0]
    rank_second = jnp.take_along_axis(rank_rows, routing[:, 1:2], axis=1)[:, 0]
    slot_first = routing[:, 0] * capacity + rank_first
    slot_second = routing[:, 1] * capacity + rank_second
    flat_out = summed_out.reshape(E * capacity, width)
    flat_grad = summed_grad.reshape(E * capacity, width)
    out_first = jnp.take(flat_out, slot_first, axis=0)
    out_second = jnp.take(flat_out, slot_second, axis=0)
    mixed = (share_first[:, None] * out_first + share_second[:, None] * out_second).astype(
        jnp.bfloat16
    )
    token_grad = (
        jnp.take(flat_grad, slot_first, axis=0) + jnp.take(flat_grad, slot_second, axis=0)
    ).astype(jnp.bfloat16)
    cot_float = cotangent.astype(jnp.float32)
    grad_first = jnp.sum(cot_float * out_first, axis=1)
    grad_second = jnp.sum(cot_float * out_second, axis=1)
    gate_grad = jnp.stack([grad_first, grad_second], axis=1)
    return (mixed, token_grad, gate_grad)


def solution(mesh):
    placed = (
        P(("groups", "dp", "expert"), None),
        P(("groups", "dp", "expert"), None),
        P(("groups", "dp", "expert"), None),
        P(("groups", "dp", "expert")),
        P(None, ("dp", "expert")),
        P(None, ("dp", "expert")),
        P(("dp", "expert"), None),
    )
    return jax.shard_map(
        on_device,
        mesh=mesh,
        in_specs=placed,
        out_specs=(
            P(("groups", "dp", "expert"), None),
            P(("groups", "dp", "expert"), None),
            P(("groups", "dp", "expert"), None),
        ),
        check_vma=False,
    )
```

profile of v0, /device:TPU:0, one launch (start us, length us, event | category | flops | bytes accessed | tf_op | source)
XLA Modules:
  0.0 149.8 jit_solution(7869169639364414181)
XLA Ops:
  0.6 0.0 copy-start
  0.6 0.8 fusion.19
  1.4 0.1 convert_convert_fusion
  1.5 0.1 convert_add_fusion
  1.6 0.7 convert_multiply_fusion.3
  2.3 0.1 fusion.12
  2.4 0.1 broadcast_in_dim.13
  2.5 0.1 convert_element_type.108
  2.6 0.7 copy.17
  3.3 7.4 %all-to-all-start.2 = ((bf16[16,1,2]{2,1,0:T(2,128)(2,1)}), bf16[16,1,2]{2,1,0:T(2,128)(2,1)S(1)}, u32[]{:S(2)}, u32[]{:S(2)}) async-start(bf16[16,1,2]{2,1,0:T(2,128)(2,1)} %copy.17), calls=%async_computation.2 | async-start | bytes 16384 | tf_op jit(solution)/shard_map/all_to_all | solution.py:58
  10.7 0.0 copy-done
  10.7 0.2 convolution_convert_fusion.2
  11.0 0.1 copy.16
  11.1 5.9 %all-to-all-done.2 = bf16[16,1,2]{2,1,0:T(2,128)(2,1)S(1)} async-done(((bf16[16,1,2]{2,1,0:T(2,128)(2,1)}), bf16[16,1,2]{2,1,0:T(2,128)(2,1)S(1)}, u32[]{:S(2)}, u32[]{:S(2)}) %all-to-all-start.2) | async-done | bytes 96 | tf_op jit(solution)/shard_map/all_to_all | solution.py:58
  17.0 0.9 broadcast_in_dim.12
  17.9 3.5 %all-to-all-start = ((bf16[16,2,4096]{2,1,0:T(2,128)(2,1)}), bf16[16,2,4096]{2,1,0:T(2,128)(2,1)S(1)}, u32[]{:S(2)}, u32[]{:S(2)}) async-start(bf16[16,2,4096]{2,1,0:T(2,128)(2,1)} %bitcast.8), calls=%async_computation | async-start | bytes 524288 | tf_op jit(solution)/shard_map/all_to_all | solution.py:56
  21.5 0.6 gather_fusion
  22.1 0.6 gather_fusion.2
  22.8 1.0 convolution_convert_fusion.1
  23.8 0.1 copy.18
  23.9 0.1 reshape.156
  24.0 7.4 %all-to-all-done = bf16[16,2,4096]{2,1,0:T(2,128)(2,1)S(1)} async-done(((bf16[16,2,4096]{2,1,0:T(2,128)(2,1)}), bf16[16,2,4096]{2,1,0:T(2,128)(2,1)S(1)}, u32[]{:S(2)}, u32[]{:S(2)}) %all-to-all-start) | async-done | bytes 262176 | tf_op jit(solution)/shard_map/all_to_all | solution.py:56
  31.5 0.9 broadcast_in_dim.17
  32.4 3.5 %all-to-all-start.3 = ((bf16[16,2,4096]{2,1,0:T(2,128)(2,1)}), bf16[16,2,4096]{2,1,0:T(2,128)(2,1)S(1)}, u32[]{:S(2)}, u32[]{:S(2)}) async-start(bf16[16,2,4096]{2,1,0:T(2,128)(2,1)} %bitcast.16), calls=%async_computation.3 | async-start | bytes 524288 | tf_op jit(solution)/shard_map/all_to_all | solution.py:57
  35.9 0.1 reshape.142
  36.0 13.5 %fusion.24 = f32[32,4096]{1,0:T(8,128)S(1)} fusion(bf16[32,4096]{1,0:T(8,128)(2,1)S(1)} %reshape.142, bf16[4096,4096]{1,0:T(8,128)(2,1)} %param.16), kind=kOutput, calls=%fused_computation.73 | convolution fusion | flops 1073741824 | bytes 34340864 | tf_op jit(solution)/shard_map/dot_general | solution.py:11
  49.5 13.5 %fusion.23 = f32[32,4096]{1,0:T(8,128)S(1)} fusion(bf16[32,4096]{1,0:T(8,128)(2,1)S(1)} %reshape.142, bf16[4096,4096]{1,0:T(8,128)(2,1)} %param.15), kind=kOutput, calls=%fused_computation.72 | convolution fusion | flops 1073741824 | bytes 34340864 | tf_op jit(solution)/shard_map/dot_general | solution.py:10
  63.1 13.6 %convolution_convert_fusion = bf16[32,4096]{1,0:T(8,128)(2,1)S(1)} fusion(bf16[4096,4096]{1,0:T(8,128)(2,1)} %param.17, f32[32,4096]{1,0:T(8,128)S(1)} %fusion.24, f32[32,4096]{1,0:T(8,128)S(1)} %fusion.23), kind=kOutput, calls=%fused_computation.9 | convolution fusion | flops 1074659328 | bytes 34865152 | tf_op jit(solution)/shard_map/dot_general | solution.py:15
  76.7 0.9 reshape.143
  77.5 0.0 all-to-all-done.3
  77.5 6.0 %all-to-all-start.1 = ((bf16[16,2,4096]{2,1,0:T(2,128)(2,1)}), bf16[16,2,4096]{2,1,0:T(2,128)(2,1)S(1)}, u32[]{:S(2)}, u32[]{:S(2)}) async-start(bf16[16,2,4096]{2,1,0:T(2,128)(2,1)} %reshape.143), calls=%async_computation.1 | async-start | bytes 524288 | tf_op jit(solution)/shard_map/all_to_all | solution.py:67
  83.5 0.1 reshape.148
  83.6 0.0 copy-start.1
  83.6 15.3 %convolution_multiply_fusion = f32[32,4096]{1,0:T(8,128)S(1)} fusion(bf16[32,4096]{1,0:T(8,128)(2,1)S(1)} %reshape.148, bf16[4096,4096]{1,0:T(8,128)(2,1)} %param.17, f32[32]{0:T(128)S(1)} %reshape.156), kind=kOutput, calls=%fused_computation.7 | convolution fusion | flops 1073872896 | bytes 34340992 | tf_op jit(solution)/shard_map/dot_general | solution.py:16
  99.0 0.0 copy-start.3
  99.0 0.0 copy-start.2
  99.0 15.4 %fusion.2 = f32[32,4096]{1,0:T(8,128)S(1)} fusion(bf16[4096,4096]{1,0:T(8,128)(2,1)} %param.15, f32[32,4096]{1,0:T(8,128)S(1)} %fusion.23, f32[32,4096]{1,0:T(8,128)S(1)} %convolution_multiply_fusion, f32[32,4096]{1,0:T(8,128)S(1)} %fusion.24), kind=kOutput, calls=%fused_computation.19 | convolution fusion | flops 1075052544 | bytes 35651584 | tf_op jit(solution)/shard_map/dot_general | solution.py:21
  114.4 15.3 %fusion = bf16[32,4096]{1,0:T(8,128)(2,1)S(1)} fusion(f32[32,4096]{1,0:T(8,128)S(1)} %fusion.2, bf16[4096,4096]{1,0:T(8,128)(2,1)} %param.16, f32[32,4096]{1,0:T(8,128)S(1)} %convolution_multiply_fusion, f32[32,4096]{1,0:T(8,128)S(1)} %fusion.23), kind=kOutput, calls=%fused_computation.8 | convolution fusion | flops 1074790400 | bytes 35389440 | tf_op jit(solution)/shard_map/dot_general | solution.py:22
  129.7 0.9 reshape.149
  130.6 0.0 all-to-all-done.1
  130.6 6.0 %all-to-all-start.4 = ((bf16[16,2,4096]{2,1,0:T(2,128)(2,1)}), bf16[16,2,4096]{2,1,0:T(2,128)(2,1)S(1)}, u32[]{:S(2)}, u32[]{:S(2)}) async-start(bf16[16,2,4096]{2,1,0:T(2,128)(2,1)} %reshape.149), calls=%async_computation.4 | async-start | bytes 524288 | tf_op jit(solution)/shard_map/all_to_all | solution.py:74
  136.6 0.0 copy-done.3
  136.6 0.3 convert_reduce_fusion.1
  136.9 0.2 reshape.146
  137.1 0.6 gather_fusion.1
  137.7 0.6 gather_fusion.3
  138.3 8.3 %all-to-all-done.4 = bf16[16,2,4096]{2,1,0:T(2,128)(2,1)S(1)} async-done(((bf16[16,2,4096]{2,1,0:T(2,128)(2,1)}), bf16[16,2,4096]{2,1,0:T(2,128)(2,1)S(1)}, u32[]{:S(2)}, u32[]{:S(2)}) %all-to-all-start.4) | async-done | bytes 262176 | tf_op jit(solution)/shard_map/all_to_all | solution.py:74
  146.6 0.3 convert_reduce_fusion
  146.9 0.2 reshape.152
  147.1 0.6 gather_fusion.5
  147.7 0.6 gather_fusion.4
  148.3 0.0 copy-done.2
  148.3 0.9 fusion.6
  149.2 0.6 pad_maximum_fusion
  149.8 0.0 copy-done.1
  (9 shorter events, 0.1 us)
Async XLA Ops:
  0.6 10.1 %copy-start = (bf16[4,4096]{1,0:T(4,128)(2,1)S(1)}, bf16[4,4096]{1,0:T(4,128)(2,1)}, u32[]{:S(2)}) copy-start(bf16[4,4096]{1,0:T(4,128)(2,1)} %param.11) | copy-start | bytes 98308
  3.3 13.7 %all-to-all-start.2 = ((bf16[16,1,2]{2,1,0:T(2,128)(2,1)}), bf16[16,1,2]{2,1,0:T(2,128)(2,1)S(1)}, u32[]{:S(2)}, u32[]{:S(2)}) async-start(bf16[16,1,2]{2,1,0:T(2,128)(2,1)} %copy.17), calls=%async_computation.2 | async-start | bytes 16384 | tf_op jit(solution)/shard_map/all_to_all | solution.py:58
  17.9 13.5 %all-to-all-start = ((bf16[16,2,4096]{2,1,0:T(2,128)(2,1)}), bf16[16,2,4096]{2,1,0:T(2,128)(2,1)S(1)}, u32[]{:S(2)}, u32[]{:S(2)}) async-start(bf16[16,2,4096]{2,1,0:T(2,128)(2,1)} %bitcast.8), calls=%async_computation | async-start | bytes 524288 | tf_op jit(solution)/shard_map/all_to_all | solution.py:56
  32.4 45.2 %all-to-all-start.3 = ((bf16[16,2,4096]{2,1,0:T(2,128)(2,1)}), bf16[16,2,4096]{2,1,0:T(2,128)(2,1)S(1)}, u32[]{:S(2)}, u32[]{:S(2)}) async-start(bf16[16,2,4096]{2,1,0:T(2,128)(2,1)} %bitcast.16), calls=%async_computation.3 | async-start | bytes 524288 | tf_op jit(solution)/shard_map/all_to_all | solution.py:57
  77.5 53.0 %all-to-all-start.1 = ((bf16[16,2,4096]{2,1,0:T(2,128)(2,1)}), bf16[16,2,4096]{2,1,0:T(2,128)(2,1)S(1)}, u32[]{:S(2)}, u32[]{:S(2)}) async-start(bf16[16,2,4096]{2,1,0:T(2,128)(2,1)} %reshape.143), calls=%async_computation.1 | async-start | bytes 524288 | tf_op jit(solution)/shard_map/all_to_all | solution.py:67
  83.6 66.2 %copy-start.1 = (bf16[4,4096]{1,0:T(4,128)(2,1)S(1)}, bf16[4,4096]{1,0:T(4,128)(2,1)}, u32[]{:S(2)}) copy-start(bf16[4,4096]{1,0:T(4,128)(2,1)} %param.11) | copy-start | bytes 98308
  99.0 37.6 %copy-start.3 = (s32[4,2]{0,1:T(2,128)S(1)}, s32[4,2]{0,1:T(2,128)}, u32[]{:S(2)}) copy-start(s32[4,2]{0,1:T(2,128)} %param.13) | copy-start | bytes 100
  99.0 49.3 %copy-start.2 = (bf16[4,4096]{1,0:T(4,128)(2,1)S(1)}, bf16[4,4096]{1,0:T(4,128)(2,1)}, u32[]{:S(2)}) copy-start(bf16[4,4096]{1,0:T(4,128)(2,1)} %param.12) | copy-start | bytes 98308
  130.6 16.1 %all-to-all-start.4 = ((bf16[16,2,4096]{2,1,0:T(2,128)(2,1)}), bf16[16,2,4096]{2,1,0:T(2,128)(2,1)S(1)}, u32[]{:S(2)}, u32[]{:S(2)}) async-start(bf16[16,2,4096]{2,1,0:T(2,128)(2,1)} %reshape.149), calls=%async_computation.4 | async-start | bytes 524288 | tf_op jit(solution)/shard_map/all_to_all | solution.py:74
where the time goes:
time: 151 us; the launch traced here: 150 us
  matrix products  87.8 us (58%)
  starting transfers between devices  26.4 us (17%)
  waiting for transfers between devices  21.7 us (14%)
  local copies, waits for them, and re-layouts  9.01 us (6%)
  other arithmetic  3.96 us (3%)
    dot_general x1, matrix products, expert_rows(): jnp.dot(d_gate, gate_weight.T, preferred_element_type=jnp.float32)  15.4 us
    dot_general x1, matrix products, expert_rows(): jnp.dot(got_dy, down_weight.T, preferred_element_type=jnp.float32)  15.3 us
    dot_general x1, matrix products, expert_rows(): jnp.dot(d_up, up_weight.T, preferred_element_type=jnp.float32)  15.3 us
    dot_general x1, matrix products, expert_rows(): part_out = jnp.dot(hidden, down_weight, preferred_element_type=jnp.float32)  13.6 us
    dot_general x1, matrix products, expert_rows(): up_pre = jnp.dot(got_x, up_weight, preferred_element_type=jnp.float32)  13.5 us
    dot_general x1, matrix products, expert_rows(): gate_pre = jnp.dot(got_x, gate_weight, preferred_element_type=jnp.float32)  13.5 us
    all_to_all x1, waiting for transfers between devices, on_device(): lax.all_to_all(part_grad.reshape(devices, capacity, width), ('dp', 'exper...  8.31 us
    all_to_all x1, waiting for transfers between devices, on_device(): lax.all_to_all(out_x, ('dp', 'expert'), split_axis=0, concat_axis=0, tile...  7.44 us
  transfers between devices with their start and end apart: 5, of which 3 were waited for; matrix products, arithmetic and copies ran while one was open for 62% of the time, Pallas kernels for 0%

commit v1 on v0

--- a/solution.py
+++ b/solution.py
@@ -1,9 +1,17 @@
+import functools
+
 import jax
 import jax.numpy as jnp
 from jax import lax
+from jax.experimental import pallas as pl
+from jax.experimental.pallas import tpu as pltpu
 from jax.sharding import PartitionSpec as P
 
 E = 8
+BLOCK = 256
+DEPTH = 7
+NN = (((1,), (0,)), ((), ()))
+NT = (((1,), (1,)), ((), ()))
 
 
 def expert_rows(got_x, got_dy, got_w, gate_weight, up_weight, down_weight):
@@ -52,33 +60,18 @@
     out_x = jnp.repeat(send_x, group_size, axis=0)
     out_dy = jnp.repeat(send_dy, group_size, axis=0)
     out_w = jnp.repeat(send_w, group_size, axis=0)
-    recv_x, recv_dy, recv_w = (
-        lax.all_to_all(out_x, ("dp", "expert"), split_axis=0, concat_axis=0, tiled=True),
-        lax.all_to_all(out_dy, ("dp", "expert"), split_axis=0, concat_axis=0, tiled=True),
-        lax.all_to_all(
-            out_w.astype(jnp.bfloat16), ("dp", "expert"), split_axis=0, concat_axis=0, tiled=True
-        ).astype(out_w.dtype),
-    )
+
+    def exchange(value):
+        return lax.all_to_all(value, ("dp", "expert"), split_axis=0, concat_axis=0, tiled=True)
+
+    recv_x, recv_dy = exchange(out_x), exchange(out_dy)
+    recv_w = exchange(out_w.astype(jnp.bfloat16)).astype(out_w.dtype)
     got_x = recv_x.reshape(devices * capacity, width)
     got_dy = recv_dy.reshape(devices * capacity, width)
     got_w = recv_w.reshape(devices * capacity)
     part_out, part_grad = expert_rows(got_x, got_dy, got_w, gate_weight, up_weight, down_weight)
-    back_out, back_grad = (
-        lax.all_to_all(
-            part_out.reshape(devices, capacity, width),
-            ("dp", "expert"),
-            split_axis=0,
-            concat_axis=0,
-            tiled=True,
-        ),
-        lax.all_to_all(
-            part_grad.reshape(devices, capacity, width),
-            ("dp", "expert"),
-            split_axis=0,
-            concat_axis=0,
-            tiled=True,
-        ),
-    )
+    back_out = exchange(part_out.reshape(devices, capacity, width))
+    back_grad = exchange(part_grad.reshape(devices, capacity, width))
     summed_out = jnp.sum(
         back_out.astype(jnp.float32).reshape(E, group_size, capacity, width), axis=1
     )
@@ -106,6 +99,284 @@
     return (mixed, token_grad, gate_grad)
 
 
+def layer_kernel(
+    n_dp,
+    route_ref,
+    first_ref,
+    x_ref,
+    dy_ref,
+    gate_hbm,
+    up_hbm,
+    down_hbm,
+    mixed_ref,
+    grad_ref,
+    score_ref,
+    gate_buf,
+    up_buf,
+    down_buf,
+    pack,
+    recv,
+    xs,
+    dys,
+    acc_out,
+    acc_grad,
+    pair_send,
+    pair_recv,
+    back_send,
+    back_recv,
+    w_sem,
+    send_sem,
+    recv_sem,
+    fsend_sem,
+    frecv_sem,
+    own_sem,
+    pair_sem,
+    bsend_sem,
+    brecv_sem,
+):
+    tok, width = x_ref.shape
+    cap = tok // 2
+    half = n_dp * cap
+    hidden = down_hbm.shape[0]
+    blocks = hidden // BLOCK
+    dp = lax.axis_index("dp")
+    core = lax.axis_index("expert")
+    other = 1 - core
+    f32, bf16 = jnp.float32, jnp.bfloat16
+
+    def weight_copies(step, slot):
+        start = pl.multiple_of(step * BLOCK, BLOCK)
+        return (
+            pltpu.make_async_copy(
+                gate_hbm.at[:, pl.ds(start, BLOCK)], gate_buf.at[slot], w_sem.at[0, slot]
+            ),
+            pltpu.make_async_copy(
+                up_hbm.at[:, pl.ds(start, BLOCK)], up_buf.at[slot], w_sem.at[1, slot]
+            ),
+            pltpu.make_async_copy(
+                down_hbm.at[pl.ds(start, BLOCK), :], down_buf.at[slot], w_sem.at[2, slot]
+            ),
+        )
+
+    def remote(src, dst, send, arrive, q, c):
+        return pltpu.make_async_remote_copy(
+            src_ref=src,
+            dst_ref=dst,
+            send_sem=send,
+            recv_sem=arrive,
+            device_id={"dp": q, "expert": c},
+            device_id_type=pl.DeviceIdType.MESH,
+        )
+
+    barrier = pltpu.get_barrier_semaphore()
+    for k in range(1, n_dp):
+        pl.semaphore_signal(
+            barrier,
+            inc=1,
+            device_id={"dp": lax.rem(dp + k, n_dp), "expert": core},
+            device_id_type=pl.DeviceIdType.MESH,
+        )
+    pl.semaphore_signal(
+        barrier,
+        inc=1,
+        device_id={"dp": dp, "expert": other},
+        device_id_type=pl.DeviceIdType.MESH,
+    )
+
+    ahead = min(DEPTH, blocks)
+    for step in range(ahead):
+        for copy in weight_copies(step, step):
+            copy.start()
+
+    slots = []
+    for t in range(tok):
+        row = []
+        for j in range(2):
+            e = route_ref[t, j]
+            rank = jnp.int32(0)
+            for s in range(t):
+                rank = rank + jnp.where((route_ref[s, 0] == e) | (route_ref[s, 1] == e), 1, 0)
+            row.append(e * cap + rank)
+        slots.append(row)
+
+    slot_rows = lax.broadcasted_iota(jnp.int32, (half, width), 0)
+    for which, ref in ((0, x_ref), (1, dy_ref)):
+        rows = ref[...].astype(f32)
+        packed = jnp.zeros((half, width), f32)
+        for t in range(tok):
+            chosen = (slot_rows == slots[t][0]) | (slot_rows == slots[t][1])
+            packed = jnp.where(chosen, jnp.broadcast_to(rows[t : t + 1, :], (half, width)), packed)
+        for e in range(n_dp):
+            pack[which, e] = packed[e * cap : (e + 1) * cap, :].astype(bf16)
+
+    pl.semaphore_wait(barrier, n_dp)
+
+    mine = core * n_dp + dp
+    sends = []
+    for k in range(1, n_dp):
+        q = lax.rem(dp + k, n_dp)
+        copy = remote(
+            pack.at[:, q], recv.at[:, mine], send_sem.at[k], recv_sem.at[k], q, core
+        )
+        copy.start()
+        sends.append(copy)
+    own = pltpu.make_async_copy(pack.at[:, dp], recv.at[:, mine], own_sem.at[0])
+    own.start()
+    forwards = [
+        remote(pack.at[:, dp], recv.at[:, mine], fsend_sem.at[0], frecv_sem.at[0], dp, other)
+    ]
+    forwards[0].start()
+    for k in range(1, n_dp):
+        slot = core * n_dp + lax.rem(dp + n_dp - k, n_dp)
+        sends[k - 1].wait_recv()
+        copy = remote(
+            recv.at[:, slot], recv.at[:, slot], fsend_sem.at[k], frecv_sem.at[k], dp, other
+        )
+        copy.start()
+        forwards.append(copy)
+    own.wait()
+    for copy in forwards:
+        copy.wait_recv()
+
+    xs[...] = recv[0].astype(f32).reshape(2 * half, width).astype(bf16)
+    dys[...] = recv[1].astype(f32).reshape(2 * half, width).astype(bf16)
+    acc_out[...] = jnp.zeros_like(acc_out)
+    acc_grad[...] = jnp.zeros_like(acc_grad)
+
+    @pl.loop(0, blocks)
+    def _(step):
+        slot = lax.rem(step, ahead)
+        for copy in weight_copies(step, slot):
+            copy.wait()
+        w_gate, w_up, w_down = gate_buf.at[slot], up_buf.at[slot], down_buf.at[slot]
+        gate_pre = lax.dot_general(xs[...], w_gate[...], NN, preferred_element_type=f32)
+        up_pre = lax.dot_general(xs[...], w_up[...], NN, preferred_element_type=f32)
+        d_hidden = lax.dot_general(dys[...], w_down[...], NT, preferred_element_type=f32)
+        sig = 1.0 / (1.0 + jnp.exp(-gate_pre))
+        silu = gate_pre * sig
+        hid = (silu * up_pre).astype(bf16)
+        d_gate = (d_hidden * up_pre * sig * (1.0 + gate_pre * (1.0 - sig))).astype(bf16)
+        d_up = (d_hidden * silu).astype(bf16)
+        acc_out[...] += lax.dot_general(hid, w_down[...], NN, preferred_element_type=f32)
+        acc_grad[...] += lax.dot_general(
+            d_gate, w_gate[...], NT, preferred_element_type=f32
+        ) + lax.dot_general(d_up, w_up[...], NT, preferred_element_type=f32)
+
+        @pl.when(step + ahead < blocks)
+        def _():
+            for copy in weight_copies(step + ahead, slot):
+                copy.start()
+
+    for copy in sends:
+        copy.wait_send()
+    for copy in forwards:
+        copy.wait_send()
+
+    keep = pl.ds(pl.multiple_of(core * half, half), half)
+    give = pl.ds(pl.multiple_of(other * half, half), half)
+    pair_send[0] = acc_out[give, :].astype(bf16)
+    pair_send[1] = acc_grad[give, :].astype(bf16)
+    pair = remote(pair_send, pair_recv, pair_sem.at[0], pair_sem.at[1], dp, other)
+    pair.start()
+    pair.wait()
+    for which, acc in ((0, acc_out), (1, acc_grad)):
+        total = acc[keep, :] + pair_recv[which].astype(f32)
+        for q in range(n_dp):
+            back_send[q, which] = total[q * cap : (q + 1) * cap, :].astype(bf16)
+    backs = []
+    for k in range(1, n_dp):
+        q = lax.rem(dp + k, n_dp)
+        copy = remote(
+            back_send.at[q], back_recv.at[dp], bsend_sem.at[k], brecv_sem.at[k], q, core
+        )
+        copy.start()
+        backs.append(copy)
+    own_back = pltpu.make_async_copy(back_send.at[dp], back_recv.at[dp], own_sem.at[1])
+    own_back.start()
+
+    row_ids = lax.broadcasted_iota(jnp.int32, (2 * tok, half), 0)
+    col_ids = lax.broadcasted_iota(jnp.int32, (2 * tok, half), 1)
+    pick = jnp.zeros((2 * tok, half), f32)
+    share_rows = lax.broadcasted_iota(jnp.int32, (tok, 1), 0)
+    share_units = jnp.zeros((tok, 1), jnp.int32)
+    for t in range(tok):
+        share_units = jnp.where(share_rows == t, first_ref[t], share_units)
+        for j in range(2):
+            chosen = (row_ids == j * tok + t) & (col_ids == slots[t][j])
+            pick = jnp.where(chosen, 1.0, pick)
+    pick = pick.astype(bf16)
+    share_first = share_units.astype(f32) / 1024.0
+    share_second = (1024 - share_units).astype(f32) / 1024.0
+
+    for copy in backs:
+        copy.wait()
+    own_back.wait()
+
+    got = back_recv[...].astype(f32)
+    got_out = got[:, 0].reshape(half, width).astype(bf16)
+    got_grad = got[:, 1].reshape(half, width).astype(bf16)
+    outs = lax.dot_general(pick, got_out, NN, preferred_element_type=f32)
+    grads = lax.dot_general(pick, got_grad, NN, preferred_element_type=f32)
+    out_first, out_second = outs[:tok], outs[tok:]
+    mixed_ref[...] = (share_first * out_first + share_second * out_second).astype(bf16)
+    grad_ref[...] = (share_first * grads[:tok] + share_second * grads[tok:]).astype(bf16)
+    cot = dy_ref[...].astype(f32)
+    score_first = jnp.sum(cot * out_first, axis=1, keepdims=True)
+    score_second = jnp.sum(cot * out_second, axis=1, keepdims=True)
+    column = lax.broadcasted_iota(jnp.int32, (tok, 2), 1)
+    score_ref[...] = jnp.where(column == 0, score_first, score_second)
+
+
+def fused(n_dp, tokens, cotangent, routing, gate_first, gate_weight, up_weight, down_weight):
+    tok, width = tokens.shape
+    cap = tok // 2
+    half = n_dp * cap
+    hidden = down_weight.shape[0]
+    f32, bf16 = jnp.float32, jnp.bfloat16
+    depth = min(DEPTH, hidden // BLOCK)
+    vmem = pl.BlockSpec(memory_space=pltpu.VMEM)
+    smem = pl.BlockSpec(memory_space=pltpu.SMEM)
+    hbm = pl.BlockSpec(memory_space=pl.ANY)
+    dma = pltpu.SemaphoreType.DMA
+    return pl.pallas_call(
+        functools.partial(layer_kernel, n_dp),
+        out_shape=(
+            jax.ShapeDtypeStruct((tok, width), bf16),
+            jax.ShapeDtypeStruct((tok, width), bf16),
+            jax.ShapeDtypeStruct((tok, 2), f32),
+        ),
+        in_specs=[smem, smem, vmem, vmem, hbm, hbm, hbm],
+        out_specs=(vmem, vmem, vmem),
+        scratch_shapes=[
+            pltpu.VMEM((depth, width, BLOCK), bf16),
+            pltpu.VMEM((depth, width, BLOCK), bf16),
+            pltpu.VMEM((depth, BLOCK, width), bf16),
+            pltpu.VMEM((2, n_dp, cap, width), bf16),
+            pltpu.VMEM((2, 2 * n_dp, cap, width), bf16),
+            pltpu.VMEM((2 * half, width), bf16),
+            pltpu.VMEM((2 * half, width), bf16),
+            pltpu.VMEM((2 * half, width), f32),
+            pltpu.VMEM((2 * half, width), f32),
+            pltpu.VMEM((2, half, width), bf16),
+            pltpu.VMEM((2, half, width), bf16),
+            pltpu.VMEM((n_dp, 2, cap, width), bf16),
+            pltpu.VMEM((n_dp, 2, cap, width), bf16),
+            dma((3, depth)),
+            dma((n_dp,)),
+            dma((n_dp,)),
+            dma((n_dp,)),
+            dma((n_dp,)),
+            dma((2,)),
+            dma((2,)),
+            dma((n_dp,)),
+            dma((n_dp,)),
+        ],
+        compiler_params=pltpu.CompilerParams(
+            collective_id=0, has_side_effects=True, vmem_limit_bytes=60 * 1024 * 1024
+        ),
+    )(routing, gate_first, tokens, cotangent, gate_weight, up_weight, down_weight)
+
+
 def solution(mesh):
     placed = (
         P(("groups", "dp", "expert"), None),
@@ -116,8 +387,10 @@
         P(None, ("dp", "expert")),
         P(("dp", "expert"), None),
     )
+    n_dp = mesh.shape["dp"]
+    one_chip = n_dp == E and mesh.shape["expert"] == 2
     return jax.shard_map(
-        on_device,
+        functools.partial(fused, n_dp) if one_chip else on_device,
         mesh=mesh,
         in_specs=placed,
         out_specs=(

time: 151 us -> 85.1 us (0.56)
  matrix products: 87.8 us -> 0 us
  Pallas kernels: 0 us -> 78.7 us
  starting transfers between devices: 26.4 us -> 0 us
  waiting for transfers between devices: 21.7 us -> 0 us
  other arithmetic: 3.96 us -> 0 us
  local copies, waits for them, and re-layouts: 9.01 us -> 5.41 us
    dot_general x8 -> x0, matrix products: 87.8 us -> none  [the longest x1 15.4 us: expert_rows(): jnp.dot(d_gate, gate_weight.T, preferred_element_type=jnp.float32)]
    pallas_call x0 -> x1, Pallas kernels: none -> 78.7 us  [fused(): pl.pallas_call(functools.partial(layer_kernel, n_dp), out_shape=(jax.Shap...]
    all_to_all x5 -> x0, starting transfers between devices: 26.4 us -> none  [the longest x1 7.39 us: on_device(): lax.all_to_all(out_w.astype(jnp.bfloat16), ('dp', 'expert'), split_axis=0...]
    all_to_all x5 -> x0, waiting for transfers between devices: 21.7 us -> none  [the longest x1 8.31 us: on_device(): lax.all_to_all(part_grad.reshape(devices, capacity, width), ('dp', 'exper...]
    unnamed x8 -> x3, local copies, waits for them, and re-layouts: 0.03 us -> 4.1 us
    gather x6 -> x0, local copies, waits for them, and re-layouts: 3.63 us -> none  [the longest x1 0.65 us: on_device(): rank_first = jnp.take_along_axis(rank_rows, routing[:, 0:1], axis=1)[:, 0]]
    reshape x6 -> x0, local copies, waits for them, and re-layouts: 2.32 us -> none  [the longest x1 0.88 us: on_device(): part_grad.reshape(devices, capacity, width)]
    broadcast_in_dim x3 -> x0, local copies, waits for them, and re-layouts: 1.87 us -> none  [the longest x1 0.9 us: on_device(): out_dy = jnp.repeat(send_dy, group_size, axis=0)]
  transfers between devices with their start and end apart: 5 -> 0, of which waited for: 3 -> 0; matrix products, arithmetic and copies ran while one was open for 62% -> 0% of each run, Pallas kernels for 0% -> 0%
where the time goes in v1:
time: 85.1 us; the launch traced here: 84.7 us
  Pallas kernels  78.7 us (92%)
  local copies, waits for them, and re-layouts  5.41 us (6%)
    pallas_call x1, Pallas kernels, fused(): pl.pallas_call(functools.partial(layer_kernel, n_dp), out_shape=(jax.Shap...  78.7 us
    unnamed x3, local copies, waits for them, and re-layouts  4.1 us

profile of v1, /device:TPU:0, one launch (start us, length us, event | category | flops | bytes accessed | tf_op | source)
XLA Modules:
  0.0 84.7 jit_solution(10853878753159071649)
XLA Ops:
  0.6 1.3 %copy.10.route_ref = s32[4,2]{1,0:T(4,128)} copy(s32[4,2]{0,1:T(2,128)} %param.9) | data formatting | bytes 64 | tf_op args[2]
  2.0 78.7 %shard_map.94 = (bf16[4,4096]{1,0:T(4,128)(2,1)}, bf16[4,4096]{1,0:T(4,128)(2,1)}, f32[4,2]{1,0:T(4,128)}) custom-call(s32[4,2]{1,0:T(4,128)} %copy.10.route_ref, s32[4]{0:T(128)} %first_ref.1, bf16[4,4096]{1,0:T(4,128)(2,1)} %x_ref.1, bf16[4,4096]{1,0:T(4,128)(2,1)} %dy_ref.1, bf16[4096,4096]{1,0:T(8,128)(2,1)} %gate_hbm.1, bf16[4096,4096]{1,0:T(8,128)(2,1)} %up_hbm.1, ...), custom_call_target="tpu_custom_call" | custom-call | tf_op jit(solution)/shard_map/pallas_call | solution.py:341
  80.6 1.3 %copy.11 = f32[4,2]{0,1:T(2,128)} copy(f32[4,2]{1,0:T(4,128)} %get-tuple-element.5) | data formatting | bytes 64 | tf_op jit(solution)/shard_map/pallas_call | solution.py:341
  81.9 1.4 %copy.14 = bf16[4,4096]{1,0:T(4,128)(2,1)} copy(bf16[4,4096]{1,0:T(4,128)(2,1)} %get-tuple-element.9) | data formatting | bytes 65536
  83.3 1.4 %copy.15 = bf16[4,4096]{1,0:T(4,128)(2,1)} copy(bf16[4,4096]{1,0:T(4,128)(2,1)} %get-tuple-element.10) | data formatting | bytes 65536

commit v2 on v1

--- a/solution.py
+++ b/solution.py
@@ -8,8 +8,8 @@
 from jax.sharding import PartitionSpec as P
 
 E = 8
-BLOCK = 256
-DEPTH = 7
+BLOCK = 512
+DEPTH = 4
 NN = (((1,), (0,)), ((), ()))
 NT = (((1,), (1,)), ((), ()))
 
@@ -111,9 +111,9 @@
     mixed_ref,
     grad_ref,
     score_ref,
-    gate_buf,
-    up_buf,
+    wide_buf,
     down_buf,
+    acts,
     pack,
     recv,
     xs,
@@ -148,10 +148,14 @@
         start = pl.multiple_of(step * BLOCK, BLOCK)
         return (
             pltpu.make_async_copy(
-                gate_hbm.at[:, pl.ds(start, BLOCK)], gate_buf.at[slot], w_sem.at[0, slot]
+                gate_hbm.at[:, pl.ds(start, BLOCK)],
+                wide_buf.at[slot, :, pl.ds(0, BLOCK)],
+                w_sem.at[0, slot],
             ),
             pltpu.make_async_copy(
-                up_hbm.at[:, pl.ds(start, BLOCK)], up_buf.at[slot], w_sem.at[1, slot]
+                up_hbm.at[:, pl.ds(start, BLOCK)],
+                wide_buf.at[slot, :, pl.ds(BLOCK, BLOCK)],
+                w_sem.at[1, slot],
             ),
             pltpu.make_async_copy(
                 down_hbm.at[pl.ds(start, BLOCK), :], down_buf.at[slot], w_sem.at[2, slot]
@@ -243,56 +247,101 @@
     acc_out[...] = jnp.zeros_like(acc_out)
     acc_grad[...] = jnp.zeros_like(acc_grad)
 
-    @pl.loop(0, blocks)
-    def _(step):
+    def inner(step):
         slot = lax.rem(step, ahead)
         for copy in weight_copies(step, slot):
             copy.wait()
-        w_gate, w_up, w_down = gate_buf.at[slot], up_buf.at[slot], down_buf.at[slot]
-        gate_pre = lax.dot_general(xs[...], w_gate[...], NN, preferred_element_type=f32)
-        up_pre = lax.dot_general(xs[...], w_up[...], NN, preferred_element_type=f32)
-        d_hidden = lax.dot_general(dys[...], w_down[...], NT, preferred_element_type=f32)
+        pre = lax.dot_general(xs[...], wide_buf[slot], NN, preferred_element_type=f32)
+        d_hidden = lax.dot_general(
+            down_buf[slot], dys[...], NT, preferred_element_type=f32
+        ).T
+        gate_pre, up_pre = pre[:, :BLOCK], pre[:, BLOCK:]
         sig = 1.0 / (1.0 + jnp.exp(-gate_pre))
         silu = gate_pre * sig
         hid = (silu * up_pre).astype(bf16)
         d_gate = (d_hidden * up_pre * sig * (1.0 + gate_pre * (1.0 - sig))).astype(bf16)
         d_up = (d_hidden * silu).astype(bf16)
-        acc_out[...] += lax.dot_general(hid, w_down[...], NN, preferred_element_type=f32)
-        acc_grad[...] += lax.dot_general(
-            d_gate, w_gate[...], NT, preferred_element_type=f32
-        ) + lax.dot_general(d_up, w_up[...], NT, preferred_element_type=f32)
-
-        @pl.when(step + ahead < blocks)
+        return hid, d_gate, d_up
+
+    def keep_acts(values):
+        for n, value in enumerate(values):
+            acts[:, n * BLOCK : (n + 1) * BLOCK] = value
+
+    def add_out(hid, slot):
+        acc_out[...] += lax.dot_general(hid, down_buf[slot], NN, preferred_element_type=f32)
+
+    def add_grad(d_both, slot):
+        acc_grad[...] += lax.dot_general(d_both, wide_buf[slot], NT, preferred_element_type=f32)
+
+    keep_acts(inner(0))
+
+    @pl.loop(1, blocks)
+    def _(step):
+        last = lax.rem(step - 1, ahead)
+        hid, d_both = acts[:, :BLOCK], acts[:, BLOCK:]
+        values = inner(step)
+        add_out(hid, last)
+        add_grad(d_both, last)
+        keep_acts(values)
+
+        @pl.when(step - 1 + ahead < blocks)
         def _():
-            for copy in weight_copies(step + ahead, slot):
+            for copy in weight_copies(step - 1 + ahead, last):
                 copy.start()
 
+    keep = pl.ds(pl.multiple_of(core * half, half), half)
+    give = pl.ds(pl.multiple_of(other * half, half), half)
+
+    def to_pair(which, acc):
+        pair_send[which] = acc[give, :].astype(bf16)
+        copy = remote(
+            pair_send.at[which],
+            pair_recv.at[which],
+            pair_sem.at[0, which],
+            pair_sem.at[1, which],
+            dp,
+            other,
+        )
+        copy.start()
+        return copy
+
+    def to_home(which, acc):
+        total = acc[keep, :] + pair_recv[which].astype(f32)
+        for q in range(n_dp):
+            back_send[which, q] = total[q * cap : (q + 1) * cap, :].astype(bf16)
+        copies = []
+        for k in range(1, n_dp):
+            q = lax.rem(dp + k, n_dp)
+            copy = remote(
+                back_send.at[which, q],
+                back_recv.at[which, dp],
+                bsend_sem.at[which, k],
+                brecv_sem.at[which, k],
+                q,
+                core,
+            )
+            copy.start()
+            copies.append(copy)
+        copy = pltpu.make_async_copy(
+            back_send.at[which, dp], back_recv.at[which, dp], own_sem.at[1 + which]
+        )
+        copy.start()
+        copies.append(copy)
+        return copies
+
+    final = (blocks - 1) % ahead
+    add_out(acts[:, :BLOCK], final)
+    pair_out = to_pair(0, acc_out)
+    add_grad(acts[:, BLOCK:], final)
+    pair_grad = to_pair(1, acc_grad)
+    pair_out.wait()
+    backs_out = to_home(0, acc_out)
+    pair_grad.wait()
+    backs_grad = to_home(1, acc_grad)
     for copy in sends:
         copy.wait_send()
     for copy in forwards:
         copy.wait_send()
-
-    keep = pl.ds(pl.multiple_of(core * half, half), half)
-    give = pl.ds(pl.multiple_of(other * half, half), half)
-    pair_send[0] = acc_out[give, :].astype(bf16)
-    pair_send[1] = acc_grad[give, :].astype(bf16)
-    pair = remote(pair_send, pair_recv, pair_sem.at[0], pair_sem.at[1], dp, other)
-    pair.start()
-    pair.wait()
-    for which, acc in ((0, acc_out), (1, acc_grad)):
-        total = acc[keep, :] + pair_recv[which].astype(f32)
-        for q in range(n_dp):
-            back_send[q, which] = total[q * cap : (q + 1) * cap, :].astype(bf16)
-    backs = []
-    for k in range(1, n_dp):
-        q = lax.rem(dp + k, n_dp)
-        copy = remote(
-            back_send.at[q], back_recv.at[dp], bsend_sem.at[k], brecv_sem.at[k], q, core
-        )
-        copy.start()
-        backs.append(copy)
-    own_back = pltpu.make_async_copy(back_send.at[dp], back_recv.at[dp], own_sem.at[1])
-    own_back.start()
 
     row_ids = lax.broadcasted_iota(jnp.int32, (2 * tok, half), 0)
     col_ids = lax.broadcasted_iota(jnp.int32, (2 * tok, half), 1)
@@ -308,23 +357,23 @@
     share_first = share_units.astype(f32) / 1024.0
     share_second = (1024 - share_units).astype(f32) / 1024.0
 
-    for copy in backs:
+    for copy in backs_out:
         copy.wait()
-    own_back.wait()
-
-    got = back_recv[...].astype(f32)
-    got_out = got[:, 0].reshape(half, width).astype(bf16)
-    got_grad = got[:, 1].reshape(half, width).astype(bf16)
+    got_out = back_recv[0].astype(f32).reshape(half, width).astype(bf16)
     outs = lax.dot_general(pick, got_out, NN, preferred_element_type=f32)
-    grads = lax.dot_general(pick, got_grad, NN, preferred_element_type=f32)
     out_first, out_second = outs[:tok], outs[tok:]
     mixed_ref[...] = (share_first * out_first + share_second * out_second).astype(bf16)
-    grad_ref[...] = (share_first * grads[:tok] + share_second * grads[tok:]).astype(bf16)
     cot = dy_ref[...].astype(f32)
     score_first = jnp.sum(cot * out_first, axis=1, keepdims=True)
     score_second = jnp.sum(cot * out_second, axis=1, keepdims=True)
     column = lax.broadcasted_iota(jnp.int32, (tok, 2), 1)
     score_ref[...] = jnp.where(column == 0, score_first, score_second)
+
+    for copy in backs_grad:
+        copy.wait()
+    got_grad = back_recv[1].astype(f32).reshape(half, width).astype(bf16)
+    grads = lax.dot_general(pick, got_grad, NN, preferred_element_type=f32)
+    grad_ref[...] = (share_first * grads[:tok] + share_second * grads[tok:]).astype(bf16)
 
 
 def fused(n_dp, tokens, cotangent, routing, gate_first, gate_weight, up_weight, down_weight):
@@ -348,9 +397,9 @@
         in_specs=[smem, smem, vmem, vmem, hbm, hbm, hbm],
         out_specs=(vmem, vmem, vmem),
         scratch_shapes=[
-            pltpu.VMEM((depth, width, BLOCK), bf16),
-            pltpu.VMEM((depth, width, BLOCK), bf16),
+            pltpu.VMEM((depth, width, 2 * BLOCK), bf16),
             pltpu.VMEM((depth, BLOCK, width), bf16),
+            pltpu.VMEM((2 * half, 3 * BLOCK), bf16),
             pltpu.VMEM((2, n_dp, cap, width), bf16),
             pltpu.VMEM((2, 2 * n_dp, cap, width), bf16),
             pltpu.VMEM((2 * half, width), bf16),
@@ -359,17 +408,17 @@
             pltpu.VMEM((2 * half, width), f32),
             pltpu.VMEM((2, half, width), bf16),
             pltpu.VMEM((2, half, width), bf16),
-            pltpu.VMEM((n_dp, 2, cap, width), bf16),
-            pltpu.VMEM((n_dp, 2, cap, width), bf16),
+            pltpu.VMEM((2, n_dp, cap, width), bf16),
+            pltpu.VMEM((2, n_dp, cap, width), bf16),
             dma((3, depth)),
             dma((n_dp,)),
             dma((n_dp,)),
             dma((n_dp,)),
             dma((n_dp,)),
-            dma((2,)),
-            dma((2,)),
-            dma((n_dp,)),
-            dma((n_dp,)),
+            dma((3,)),
+            dma((2, 2)),
+            dma((2, n_dp)),
+            dma((2, n_dp)),
         ],
         compiler_params=pltpu.CompilerParams(
             collective_id=0, has_side_effects=True, vmem_limit_bytes=60 * 1024 * 1024

time: 85.1 us -> 73.1 us (0.86)
  Pallas kernels: 78.7 us -> 66.6 us
    pallas_call x1, Pallas kernels: 78.7 us -> 66.6 us  [fused(): pl.pallas_call(functools.partial(layer_kernel, n_dp), out_shape=(jax.Shap...]
where the time goes in v2:
time: 73.1 us; the launch traced here: 72.7 us
  Pallas kernels  66.6 us (91%)
  local copies, waits for them, and re-layouts  5.41 us (7%)
    pallas_call x1, Pallas kernels, fused(): pl.pallas_call(functools.partial(layer_kernel, n_dp), out_shape=(jax.Shap...  66.6 us
    unnamed x3, local copies, waits for them, and re-layouts  4.1 us

profile of v2, /device:TPU:0, one launch (start us, length us, event | category | flops | bytes accessed | tf_op | source)
XLA Modules:
  0.0 72.7 jit_solution(15232095184518992809)
XLA Ops:
  0.6 1.3 %copy.10.route_ref = s32[4,2]{1,0:T(4,128)} copy(s32[4,2]{0,1:T(2,128)} %param.9) | data formatting | bytes 64 | tf_op args[2]
  2.0 66.6 %shard_map.94 = (bf16[4,4096]{1,0:T(4,128)(2,1)}, bf16[4,4096]{1,0:T(4,128)(2,1)}, f32[4,2]{1,0:T(4,128)}) custom-call(s32[4,2]{1,0:T(4,128)} %copy.10.route_ref, s32[4]{0:T(128)} %first_ref.1, bf16[4,4096]{1,0:T(4,128)(2,1)} %x_ref.1, bf16[4,4096]{1,0:T(4,128)(2,1)} %dy_ref.1, bf16[4096,4096]{1,0:T(8,128)(2,1)} %gate_hbm.1, bf16[4096,4096]{1,0:T(8,128)(2,1)} %up_hbm.1, ...), custom_call_target="tpu_custom_call" | custom-call | tf_op jit(solution)/shard_map/pallas_call | solution.py:390
  68.6 1.3 %copy.11 = f32[4,2]{0,1:T(2,128)} copy(f32[4,2]{1,0:T(4,128)} %get-tuple-element.5) | data formatting | bytes 64 | tf_op jit(solution)/shard_map/pallas_call | solution.py:390
  69.9 1.4 %copy.14 = bf16[4,4096]{1,0:T(4,128)(2,1)} copy(bf16[4,4096]{1,0:T(4,128)(2,1)} %get-tuple-element.9) | data formatting | bytes 65536
  71.3 1.4 %copy.15 = bf16[4,4096]{1,0:T(4,128)(2,1)} copy(bf16[4,4096]{1,0:T(4,128)(2,1)} %get-tuple-element.10) | data formatting | bytes 65536
